TPU v7x, 32 devices: a whole 2x2x4 slice. The times are simulated.
32 devices in a mesh: group: 1, expert: 16 (over z, y, x), step: 2 (over core).
Axes of the slice: x: 2, y: 2, z: 4, core: 2. Of those that a mesh axis runs over, the one named last changes fastest.
Arguments:
- latents: float32 [2, 2048, 1536], P('step', ('group', 'expert')), may hold values from -6 to 6
- modulation: float32 [2, 6, 1536], P('group'), may hold values from -3 to 3
- shallow_routes: int32 [2, 2048, 2], P('step', ('group', 'expert')), may hold values from 0 to 3, all different within a row; in each aligned block of 128 rows (0 to 127, 128 to 255, ..., all dimensions but the last counted through in order) at most 64 rows name the same one
- deep_routes: int32 [2048, 2], P(('group', 'expert')), may hold values from 0 to 3, all different within a row; in each aligned block of 128 rows (0 to 127, 128 to 255, ...) at most 64 rows name the same one
- refresh: int32 [16], P(('group', 'expert')), may hold values from 0 to 1
- shallow_in: bfloat16 [16, 1536, 768], P('expert'), may hold values from -0.15625 to 0.15625
- shallow_out: bfloat16 [16, 768, 1536], P('expert'), may hold values from -0.109375 to 0.109375
- deep_in: bfloat16 [16, 1536, 768], P('expert'), may hold values from -0.15625 to 0.15625
- deep_out: bfloat16 [16, 768, 1536], P('expert'), may hold values from -0.109375 to 0.109375
- shallow_router: float32 [1536, 4], replicated, may hold values from -0.15625 to 0.15625
- deep_router: float32 [1536, 4], replicated, may hold values from -0.15625 to 0.15625
Outputs:
- result: bfloat16 [2, 2048, 1536], P('step', ('group', 'expert'))
Inputs may be any that keep to these rules, and one draw needn't show every extreme that they name: `shallow_routes`: within the 128 rows of one index of expert (aligned blocks), each expert is named by at most 64 rows, and by exactly 64 rows in some block; a row names two different experts. `deep_routes`: within the 128 rows of one index of expert (aligned blocks), each expert is named by at most 64 rows, and by exactly 64 rows in some block; a row names two different experts.
All inputs are finite; a program needn't handle non-finite values.
Results may differ from a plain program's by a relative error of at most 0.01.
Values may be sent and summed in bfloat16 or wider, within the bound.
No kernel may reach another device: no remote copies, remote signals or barrier semaphores. Data moves between devices by JAX's collectives and lax.ppermute only.
A program may use at most 64 MiB of HBM per device.

v0:
```python
import jax
import jax.numpy as jnp
from jax import lax
from jax.sharding import PartitionSpec as P


def from_root(block, axis, owner):
    block = jnp.where(lax.axis_index(axis) == owner, block, jnp.zeros_like(block))
    return lax.psum(block, axis)


def modulate(hidden, shift_row, scale_row):
    average = jnp.mean(hidden, axis=-1, keepdims=True)
    centred = hidden - average
    variance = jnp.mean(centred * centred, axis=-1, keepdims=True)
    return (centred * lax.rsqrt(variance + 1e-06) * (1.0 + scale_row) + shift_row).astype(
        jnp.bfloat16
    )


def plan(normed, routes, router, capacity):
    rows_count, width = normed.shape
    experts = router.shape[1]
    logits = jnp.dot(normed.astype(jnp.float32), router, precision=lax.Precision.HIGHEST)
    hits = routes[:, :, None] == jnp.arange(experts, dtype=jnp.int32)
    chosen = jnp.sum(jnp.where(hits, logits[:, None, :], 0.0), axis=-1)
    gate_sig = jax.nn.sigmoid(chosen)
    weights = gate_sig / jnp.sum(gate_sig, axis=-1, keepdims=True)
    pair_hits = hits.reshape(rows_count * 2, experts).astype(jnp.int32)
    position = jnp.sum(pair_hits * (jnp.cumsum(pair_hits, axis=0) - 1), axis=-1).reshape(
        rows_count, 2
    )
    slot_hit = position[:, :, None] == jnp.arange(capacity, dtype=jnp.int32)
    placed = hits[:, :, :, None] & slot_hit[:, :, None, :]
    dispatch = jnp.any(placed, axis=1).reshape(rows_count, experts * capacity).astype(jnp.bfloat16)
    gathered = jnp.einsum("rs,rd->sd", dispatch, normed, preferred_element_type=jnp.float32).astype(
        jnp.bfloat16
    )
    combine_w = jnp.sum(jnp.where(placed, weights[:, :, None, None], 0.0), axis=1)
    return (gathered.reshape(experts, capacity, width), combine_w)


def spread(gathered, slices):
    experts, capacity, width = gathered.shape
    quarters = slices // experts
    return jnp.broadcast_to(gathered[:, None], (experts, quarters, capacity, width)).reshape(
        slices, capacity, width
    )


def expert_rows(piece, weight_in, weight_out):
    dims = piece.shape
    flat_rows = piece.reshape(-1, dims[-1])
    hidden = jax.nn.gelu(
        jnp.dot(flat_rows, weight_in, preferred_element_type=jnp.float32), approximate=True
    ).astype(jnp.bfloat16)
    return (
        jnp.dot(hidden, weight_out, preferred_element_type=jnp.float32)
        .astype(jnp.bfloat16)
        .reshape(dims)
    )


def combine(summed, combine_w):
    rows_count = combine_w.shape[0]
    width = summed.shape[-1]
    return jnp.dot(
        combine_w.reshape(rows_count, -1),
        summed.reshape(-1, width),
        precision=lax.Precision.HIGHEST,
        preferred_element_type=jnp.float32,
    )


def finish(returned, combine_w):
    experts = combine_w.shape[1]
    width = returned.shape[2]
    summed = jnp.sum(
        returned.astype(jnp.float32).reshape(experts, -1, returned.shape[1], width), axis=1
    )
    return combine(summed, combine_w)


def body(
    latents,
    modulation,
    shallow_routes,
    deep_routes,
    refresh,
    shallow_in,
    shallow_out,
    deep_in,
    deep_out,
    shallow_router,
    deep_router,
):
    slices = lax.axis_size("expert")
    experts = shallow_router.shape[1]
    rows_count = latents.shape[1]
    capacity = 2 * max(rows_count * 5 // 64, rows_count // experts)
    step_idx = lax.axis_index("step")
    root_idx = refresh[0]
    own_mod = lax.dynamic_index_in_dim(modulation, step_idx, 0, keepdims=False)
    features = latents[0]
    normed = modulate(features, own_mod[0], own_mod[1])
    gathered, combine_w = plan(normed, shallow_routes[0], shallow_router, capacity)
    partial_value = expert_rows(
        lax.all_to_all(spread(gathered, slices), "expert", split_axis=0, concat_axis=0, tiled=True),
        shallow_in[0],
        shallow_out[0],
    )
    returned = lax.all_to_all(partial_value, "expert", split_axis=0, concat_axis=0, tiled=True)
    moe_shallow = finish(returned, combine_w)
    after_shallow = (features + own_mod[2] * moe_shallow).astype(jnp.bfloat16)
    normed_deep = modulate(after_shallow.astype(jnp.float32), own_mod[3], own_mod[4])
    gathered_deep, combine_deep = plan(normed_deep, deep_routes, deep_router, capacity)
    partial_value = expert_rows(
        lax.all_to_all(
            spread(gathered_deep, slices), "expert", split_axis=0, concat_axis=0, tiled=True
        ),
        deep_in[0],
        deep_out[0],
    )
    returned_deep = lax.all_to_all(partial_value, "expert", split_axis=0, concat_axis=0, tiled=True)
    moe_deep = finish(returned_deep, combine_deep)
    own_delta = (own_mod[5] * moe_deep).astype(jnp.bfloat16)
    deep_delta = from_root(own_delta, "step", root_idx)
    result = (after_shallow.astype(jnp.float32) + deep_delta.astype(jnp.float32)).astype(
        jnp.bfloat16
    )
    return result[None]


def solution(mesh):
    in_specs = (
        P("step", ("group", "expert"), None),
        P("group", None, None),
        P("step", ("group", "expert"), None),
        P(("group", "expert"), None),
        P(("group", "expert")),
        P("expert", None, None),
        P("expert", None, None),
        P("expert", None, None),
        P("expert", None, None),
        P(),
        P(),
    )
    out_specs = P("step", ("group", "expert"), None)
    return jax.shard_map(body, mesh=mesh, in_specs=in_specs, out_specs=out_specs, check_vma=False)
```

profile of v0, /device:TPU:0, one launch (start us, length us, event | category | flops | bytes accessed | tf_op | source)
XLA Modules:
  0.0 376.2 jit_solution(6678324923360058093)
XLA Ops:
  6.5 0.9 copy.32
  7.5 0.1 eq.123
  7.6 0.1 eq.119
  7.8 1.3 reduce_sum.127
  9.0 1.4 multiply_reduce_fusion.1
  10.4 0.7 iota_compare_fusion.5
  11.1 1.2 reduce-window.14
  12.3 0.1 slice.46
  12.4 0.1 copy.34
  12.5 0.1 copy.35
  12.6 0.1 add_bitcast_fusion.1
  12.7 0.1 eq.127
  12.9 0.1 copy.36
  13.0 0.9 dynamic-slice_reduce_fusion.1
  13.9 1.6 convolution_convert_fusion.3
  15.6 0.3 broadcast_in_dim.82
  15.9 79.5 %all_to_all.20 = bf16[16,64,1536]{2,1,0:T(8,128)(2,1)} all-to-all(bf16[16,64,1536]{2,1,0:T(8,128)(2,1)S(1)} %bitcast.112), channel_id=1, replica_groups=mesh['group'=1,'expert'=16,'step'=2] {'expert'}, dimensions={0} | all-to-all | bytes 6291456 | tf_op jit(solution)/shard_map/all_to_all | solution.py:108
  95.4 10.4 %convolution_convert_fusion.1 = bf16[1024,1536]{1,0:T(8,128)(2,1)} fusion(bf16[1,768,1536]{2,1,0:T(8,128)(2,1)S(1)} %copy-done, bf16[1024,1536]{1,0:T(8,128)(2,1)} %bitcast.116, bf16[1,1536,768]{2,1,0:T(8,128)(2,1)} %param.16), kind=kOutput, calls=%fused_computation.5 | convolution fusion | flops 4840488960 | bytes 11010048 | tf_op jit(solution)/shard_map/dot_general | solution.py:58
  105.8 4.6 %all-to-all-start.1 = ((bf16[16,64,1536]{2,1,0:T(8,128)(2,1)}), bf16[16,64,1536]{2,1,0:T(8,128)(2,1)}, u32[]{:S(2)}, u32[]{:S(2)}) async-start(bf16[16,64,1536]{2,1,0:T(8,128)(2,1)} %bitcast.114), calls=%async_computation.1 | async-start | bytes 6291456 | tf_op jit(solution)/shard_map/all_to_all | solution.py:112
  110.5 0.1 copy.37
  110.6 0.1 eq.139
  110.7 0.1 eq.135
  110.9 1.2 reduce-window.16
  112.1 0.1 slice.47
  112.2 0.1 copy.39
  112.3 0.1 copy.40
  112.4 0.1 add_bitcast_fusion
  112.5 0.1 eq.143
  112.7 0.1 copy.41
  112.7 0.5 fusion.44
  113.5 57.2 %all-to-all-done.1 = bf16[16,64,1536]{2,1,0:T(8,128)(2,1)} async-done(((bf16[16,64,1536]{2,1,0:T(8,128)(2,1)}), bf16[16,64,1536]{2,1,0:T(8,128)(2,1)}, u32[]{:S(2)}, u32[]{:S(2)}) %all-to-all-start.1) | async-done | bytes 3145760 | tf_op jit(solution)/shard_map/all_to_all | solution.py:112
  170.7 2.6 convert_reduce_fusion.1
  173.2 1.1 fusion.61
  174.3 0.2 multiply_reduce_fusion
  174.6 0.2 add_convert_fusion.1
  174.8 0.3 convolution_convert_fusion.2
  175.1 0.1 copy-done.2
  175.2 0.3 broadcast_in_dim.86
  175.5 84.7 %all_to_all.21 = bf16[16,64,1536]{2,1,0:T(8,128)(2,1)} all-to-all(bf16[16,64,1536]{2,1,0:T(8,128)(2,1)S(1)} %bitcast.113), channel_id=1, replica_groups=mesh['group'=1,'expert'=16,'step'=2] {'expert'}, dimensions={0} | all-to-all | bytes 6291456 | tf_op jit(solution)/shard_map/all_to_all | solution.py:118
  260.3 11.1 %convolution_convert_fusion = bf16[1024,1536]{1,0:T(8,128)(2,1)} fusion(bf16[1,768,1536]{2,1,0:T(8,128)(2,1)} %param.19, bf16[1024,1536]{1,0:T(8,128)(2,1)} %bitcast.117, bf16[1,1536,768]{2,1,0:T(8,128)(2,1)} %param.18), kind=kOutput, calls=%fused_computation.4 | convolution fusion | flops 4840488960 | bytes 11010048 | tf_op jit(solution)/shard_map/dot_general | solution.py:58
  271.4 4.6 %all-to-all-start.3 = ((bf16[16,64,1536]{2,1,0:T(8,128)(2,1)}), bf16[16,64,1536]{2,1,0:T(8,128)(2,1)}, u32[]{:S(2)}, u32[]{:S(2)}) async-start(bf16[16,64,1536]{2,1,0:T(8,128)(2,1)} %bitcast.115), calls=%async_computation.3 | async-start | bytes 6291456 | tf_op jit(solution)/shard_map/all_to_all | solution.py:124
  276.7 0.4 fusion.62
  277.2 0.1 fusion.46
  277.3 58.9 %all-to-all-done.3 = bf16[16,64,1536]{2,1,0:T(8,128)(2,1)} async-done(((bf16[16,64,1536]{2,1,0:T(8,128)(2,1)}), bf16[16,64,1536]{2,1,0:T(8,128)(2,1)}, u32[]{:S(2)}, u32[]{:S(2)}) %all-to-all-start.3) | async-done | bytes 3145760 | tf_op jit(solution)/shard_map/all_to_all | solution.py:124
  336.2 2.6 convert_reduce_fusion
  338.7 1.7 fusion.22
  340.5 27.0 %all-reduce.2.cloned.1.call-done = bf16[128,1536]{1,0:T(8,128)(2,1)} async-done(((bf16[128,1536]{1,0:T(8,128)(2,1)}), bf16[128,1536]{1,0:T(8,128)(2,1)}) %all-reduce.2.cloned.1.call-update) | async-done | bytes 393232 | tf_op jit(solution)/shard_map/psum | solution.py:9
  367.6 1.8 fusion.39
  (41 shorter events, 0.5 us)
Async XLA Ops:
  6.5 88.8 %copy-start = (bf16[1,768,1536]{2,1,0:T(8,128)(2,1)S(1)}, bf16[1,768,1536]{2,1,0:T(8,128)(2,1)}, u32[]{:S(2)}) copy-start(bf16[1,768,1536]{2,1,0:T(8,128)(2,1)} %param.17) | copy-start | bytes 7077892
  105.8 4.7 %copy-start.7 = (s32[128,2]{0,1:T(2,128)S(1)}, s32[128,2]{0,1:T(2,128)}, u32[]{:S(2)}) copy-start(s32[128,2]{0,1:T(2,128)} %param.14) | copy-start | bytes 3076
  105.8 6.9 %copy-start.1 = (f32[1,128,1536]{2,1,0:T(8,128)S(1)}, f32[1,128,1536]{2,1,0:T(8,128)}, u32[]{:S(2)}) copy-start(f32[1,128,1536]{2,1,0:T(8,128)} %param.11) | copy-start | bytes 2359300
  105.8 6.9 %copy-start.4 = (f32[1536,4]{0,1:T(4,128)S(1)}, f32[1536,4]{0,1:T(4,128)}, u32[]{:S(2)}) copy-start(f32[1536,4]{0,1:T(4,128)} %param.20) | copy-start | bytes 73732
  105.8 7.4 %copy-start.6 = (s32[1,128,2]{1,2,0:T(2,128)S(1)}, s32[1,128,2]{1,2,0:T(2,128)}, u32[]{:S(2)}) copy-start(s32[1,128,2]{1,2,0:T(2,128)} %param.13) | copy-start | bytes 3076
  105.8 64.8 %all-to-all-start.1 = ((bf16[16,64,1536]{2,1,0:T(8,128)(2,1)}), bf16[16,64,1536]{2,1,0:T(8,128)(2,1)}, u32[]{:S(2)}, u32[]{:S(2)}) async-start(bf16[16,64,1536]{2,1,0:T(8,128)(2,1)} %bitcast.114), calls=%async_computation.1 | async-start | bytes 6291456 | tf_op jit(solution)/shard_map/all_to_all | solution.py:112
  174.3 0.9 copy-start.2
  271.4 5.3 %copy-start.5 = (f32[1536,4]{0,1:T(4,128)S(1)}, f32[1536,4]{0,1:T(4,128)}, u32[]{:S(2)}) copy-start(f32[1536,4]{0,1:T(4,128)} %param.21) | copy-start | bytes 73732
  271.4 64.8 %all-to-all-start.3 = ((bf16[16,64,1536]{2,1,0:T(8,128)(2,1)}), bf16[16,64,1536]{2,1,0:T(8,128)(2,1)}, u32[]{:S(2)}, u32[]{:S(2)}) async-start(bf16[16,64,1536]{2,1,0:T(8,128)(2,1)} %bitcast.115), calls=%async_computation.3 | async-start | bytes 6291456 | tf_op jit(solution)/shard_map/all_to_all | solution.py:124
  276.0 91.6 %all-reduce.2.cloned.1.call-start = ((), (), s32[]{:S(2)}) async-start(), calls=%async_computation.4 | async-start | bytes 786432 | tf_op jit(solution)/shard_map/psum | solution.py:9
  277.3 90.3 %copy-start.3 = (f32[128,1536]{1,0:T(8,128)S(1)}, f32[128,1536]{1,0:T(8,128)}, u32[]{:S(2)}) copy-start(f32[128,1536]{1,0:T(8,128)} %copy-done.2) | copy-start | bytes 2359300
Sparse Core Ops, SparseCore 0:
  340.6 26.8 all-reduce.1
where the time goes:
time: 377 us; the launch traced here: 376 us
  blocking collectives  164 us (44%)
  waiting for transfers between devices  143 us (38%)
  matrix products  27.3 us (7%)
  other arithmetic  14.7 us (4%)
  between operations  14.3 us (4%)
  starting transfers between devices  9.3 us (2%)
    all_to_all x2, waiting for transfers between devices, body(): lax.all_to_all(partial_value, 'expert', split_axis=0, concat_axis=0, tile...  116 us
    all_to_all x1, blocking collectives, body(): lax.all_to_all(spread(gathered_deep, slices), 'expert', split_axis=0, con...  84.7 us
    all_to_all x1, blocking collectives, body(): lax.all_to_all(spread(gathered, slices), 'expert', split_axis=0, concat_a...  79.5 us
    psum x1, waiting for transfers between devices, from_root(): return lax.psum(block, axis)  27 us
    dot_general x2, matrix products, expert_rows(): jnp.dot(hidden, weight_out, preferred_element_type=jnp.float32)  21.5 us
    all_to_all x2, starting transfers between devices, body(): lax.all_to_all(partial_value, 'expert', split_axis=0, concat_axis=0, tile...  9.25 us
  transfers between devices with their start and end apart: 3, of which 3 were waited for; matrix products, arithmetic and copies ran while one was open for 1% of the time, Pallas kernels for 0%

commit v1 on v0

--- a/solution.py
+++ b/solution.py
@@ -2,6 +2,18 @@
 import jax.numpy as jnp
 from jax import lax
 from jax.sharding import PartitionSpec as P
+
+
+def sent_to_each(value, axis, split, join):
+    ways, here = (lax.axis_size(axis), lax.axis_index(axis))
+    width = value.shape[split] // ways
+    turned = jnp.roll(value, -here * width, axis=split)
+    got = [lax.slice_in_dim(turned, 0, width, axis=split)]
+    for far in range(1, ways):
+        sent = lax.slice_in_dim(turned, far * width, (far + 1) * width, axis=split)
+        got.append(lax.ppermute(sent, axis, [(d, (d + far) % ways) for d in range(ways)]))
+    line = jnp.concatenate(got[::-1], axis=join)
+    return jnp.roll(line, (here + 1) * got[0].shape[join], axis=join)
 
 
 def from_root(block, axis, owner):
@@ -115,11 +127,7 @@
     normed_deep = modulate(after_shallow.astype(jnp.float32), own_mod[3], own_mod[4])
     gathered_deep, combine_deep = plan(normed_deep, deep_routes, deep_router, capacity)
     partial_value = expert_rows(
-        lax.all_to_all(
-            spread(gathered_deep, slices), "expert", split_axis=0, concat_axis=0, tiled=True
-        ),
-        deep_in[0],
-        deep_out[0],
+        sent_to_each(spread(gathered_deep, slices), "expert", 0, 0), deep_in[0], deep_out[0]
     )
     returned_deep = lax.all_to_all(partial_value, "expert", split_axis=0, concat_axis=0, tiled=True)
     moe_deep = finish(returned_deep, combine_deep)

time: 377 us -> 417 us (1.11)
  blocking collectives: 164 us -> 79.5 us
  starting transfers between devices: 9.3 us -> 73 us
  waiting for transfers between devices: 143 us -> 193 us
  local copies, waits for them, and re-layouts: 3.26 us -> 9.5 us
  other arithmetic: 14.7 us -> 19.2 us
    all_to_all x1 -> x0, blocking collectives: 84.7 us -> none  [body(): lax.all_to_all(spread(gathered_deep, slices), 'expert', split_axis=0, con...]
    ppermute x0 -> x15, starting transfers between devices: none -> 63.7 us  [sent_to_each(): lax.ppermute(sent, axis, [(d, (d + far) % ways) for d in range(ways)])]
    ppermute x0 -> x15, waiting for transfers between devices: none -> 54.9 us  [sent_to_each(): lax.ppermute(sent, axis, [(d, (d + far) % ways) for d in range(ways)])]
  transfers between devices with their start and end apart: 3 -> 18, of which waited for: 3 -> 13; matrix products, arithmetic and copies ran while one was open for 1% -> 1% of each run, Pallas kernels for 0% -> 0%
where the time goes in v1:
time: 417 us; the launch traced here: 416 us
  waiting for transfers between devices  193 us (46%)
  blocking collectives  79.5 us (19%)
  starting transfers between devices  73 us (18%)
  matrix products  27.3 us (7%)
  other arithmetic  19.2 us (5%)
  between operations  14.5 us (3%)
  local copies, waits for them, and re-layouts  9.5 us (2%)
    all_to_all x2, waiting for transfers between devices, body(): lax.all_to_all(partial_value, 'expert', split_axis=0, concat_axis=0, tile...  112 us
    all_to_all x1, blocking collectives, body(): lax.all_to_all(spread(gathered, slices), 'expert', split_axis=0, concat_a...  79.5 us
    ppermute x15, starting transfers between devices, sent_to_each(): lax.ppermute(sent, axis, [(d, (d + far) % ways) for d in range(ways)])  63.7 us
    ppermute x15, waiting for transfers between devices, sent_to_each(): lax.ppermute(sent, axis, [(d, (d + far) % ways) for d in range(ways)])  54.9 us
    psum x1, waiting for transfers between devices, from_root(): return lax.psum(block, axis)  26.3 us
    dot_general x2, matrix products, expert_rows(): jnp.dot(hidden, weight_out, preferred_element_type=jnp.float32)  21.5 us
    all_to_all x2, starting transfers between devices, body(): lax.all_to_all(partial_value, 'expert', split_axis=0, concat_axis=0, tile...  9.25 us
  transfers between devices with their start and end apart: 18, of which 13 were waited for; matrix products, arithmetic and copies ran while one was open for 1% of the time, Pallas kernels for 0%

profile of v1, /device:TPU:0, one launch (start us, length us, event | category | flops | bytes accessed | tf_op | source)
XLA Modules:
  0.0 416.4 jit_solution(5347170742602002612)
XLA Ops:
  6.5 0.9 copy.32
  8.8 1.3 reduce_sum.127
  10.1 1.4 multiply_reduce_fusion.1
  12.2 1.2 reduce-window.14
  13.8 1.2 reduce-window.16
  15.7 1.5 dynamic-slice_reduce_fusion.1
  17.2 1.6 convolution_convert_fusion.3
  19.1 79.5 %all_to_all.15 = bf16[16,64,1536]{2,1,0:T(8,128)(2,1)} all-to-all(bf16[16,64,1536]{2,1,0:T(8,128)(2,1)S(1)} %bitcast.113), channel_id=1, replica_groups=mesh['group'=1,'expert'=16,'step'=2] {'expert'}, dimensions={0} | all-to-all | bytes 6291456 | tf_op jit(solution)/shard_map/all_to_all | solution.py:120
  98.7 10.4 %convolution_convert_fusion.1 = bf16[1024,1536]{1,0:T(8,128)(2,1)} fusion(bf16[1,768,1536]{2,1,0:T(8,128)(2,1)S(1)} %copy-done, bf16[1024,1536]{1,0:T(8,128)(2,1)} %bitcast.117, bf16[1,1536,768]{2,1,0:T(8,128)(2,1)} %param.18), kind=kOutput, calls=%fused_computation.9 | convolution fusion | flops 4840488960 | bytes 11010048 | tf_op jit(solution)/shard_map/dot_general | solution.py:70
  109.1 4.6 %all-to-all-start.1 = ((bf16[16,64,1536]{2,1,0:T(8,128)(2,1)}), bf16[16,64,1536]{2,1,0:T(8,128)(2,1)}, u32[]{:S(2)}, u32[]{:S(2)}) async-start(bf16[16,64,1536]{2,1,0:T(8,128)(2,1)} %bitcast.114), calls=%async_computation.1 | async-start | bytes 6291456 | tf_op jit(solution)/shard_map/all_to_all | solution.py:124
  115.2 58.8 %all-to-all-done.1 = bf16[16,64,1536]{2,1,0:T(8,128)(2,1)} async-done(((bf16[16,64,1536]{2,1,0:T(8,128)(2,1)}), bf16[16,64,1536]{2,1,0:T(8,128)(2,1)}, u32[]{:S(2)}, u32[]{:S(2)}) %all-to-all-start.1) | async-done | bytes 3145760 | tf_op jit(solution)/shard_map/all_to_all | solution.py:124
  173.9 2.6 convert_reduce_fusion.1
  176.5 1.1 fusion.64
  178.8 1.1 fusion.17
  179.9 1.7 copy-done.2
  181.6 1.3 fusion.63
  182.9 12.5 %collective-permute-start = (bf16[1,64,1536]{2,1,0:T(8,128)(2,1)}, bf16[1,64,1536]{2,1,0:T(8,128)(2,1)}, u32[]{:S(2)}, u32[]{:S(2)}) collective-permute-start(bf16[1,64,1536]{2,1,0:T(8,128)(2,1)} %get-tuple-element.26), channel_id=1, source_target_pairs={{0,30},{2,0},{4,2},{6,4},{8,6},{10,8},{12,10},{14,12},{16,14},{18,... | collective-permute-start | bytes 589832 | tf_op jit(solution)/shard_map/ppermute | solution.py:14
  195.5 2.6 collective-permute-start.12
  198.1 2.0 collective-permute-start.11
  200.1 4.7 %collective-permute-start.1 = (bf16[1,64,1536]{2,1,0:T(8,128)(2,1)}, bf16[1,64,1536]{2,1,0:T(8,128)(2,1)S(1)}, u32[]{:S(2)}, u32[]{:S(2)}) collective-permute-start(bf16[1,64,1536]{2,1,0:T(8,128)(2,1)} %get-tuple-element.25), channel_id=1, source_target_pairs={{0,28},{2,30},{4,0},{6,2},{8,4},{10,6},{12,8},{14,10},{16,12},{18,... | collective-permute-start | bytes 589832 | tf_op jit(solution)/shard_map/ppermute | solution.py:14
  204.8 0.9 constant_dynamic-update-slice_fusion.14
  205.7 4.7 %collective-permute-done.1 = bf16[1,64,1536]{2,1,0:T(8,128)(2,1)S(1)} collective-permute-done((bf16[1,64,1536]{2,1,0:T(8,128)(2,1)}, bf16[1,64,1536]{2,1,0:T(8,128)(2,1)S(1)}, u32[]{:S(2)}, u32[]{:S(2)}) %collective-permute-start.1) | collective-permute-done | bytes 196640 | tf_op jit(solution)/shard_map/ppermute | solution.py:14
  210.4 4.0 collective-permute-start.2
  214.5 4.6 %collective-permute-done.2 = bf16[1,64,1536]{2,1,0:T(8,128)(2,1)S(1)} collective-permute-done((bf16[1,64,1536]{2,1,0:T(8,128)(2,1)}, bf16[1,64,1536]{2,1,0:T(8,128)(2,1)S(1)}, u32[]{:S(2)}, u32[]{:S(2)}) %collective-permute-start.2) | collective-permute-done | bytes 196640 | tf_op jit(solution)/shard_map/ppermute | solution.py:14
  219.1 2.4 collective-permute-start.3
  221.5 3.8 collective-permute-done.3
  225.2 3.2 collective-permute-start.4
  228.5 3.6 collective-permute-done.4
  232.0 3.6 collective-permute-start.5
  235.6 3.6 collective-permute-done.5
  239.2 12.3 %collective-permute-start.6 = (bf16[1,64,1536]{2,1,0:T(8,128)(2,1)}, bf16[1,64,1536]{2,1,0:T(8,128)(2,1)S(1)}, u32[]{:S(2)}, u32[]{:S(2)}) collective-permute-start(bf16[1,64,1536]{2,1,0:T(8,128)(2,1)} %get-tuple-element.20), channel_id=1, source_target_pairs={{0,18},{2,20},{4,22},{6,24},{8,26},{10,28},{12,30},{14,0},{16,2},{... | collective-permute-start | bytes 589832 | tf_op jit(solution)/shard_map/ppermute | solution.py:14
  251.6 4.8 %collective-permute-done.6 = bf16[1,64,1536]{2,1,0:T(8,128)(2,1)S(1)} collective-permute-done((bf16[1,64,1536]{2,1,0:T(8,128)(2,1)}, bf16[1,64,1536]{2,1,0:T(8,128)(2,1)S(1)}, u32[]{:S(2)}, u32[]{:S(2)}) %collective-permute-start.6) | collective-permute-done | bytes 196640 | tf_op jit(solution)/shard_map/ppermute | solution.py:14
  256.4 7.1 %collective-permute-start.7 = (bf16[1,64,1536]{2,1,0:T(8,128)(2,1)}, bf16[1,64,1536]{2,1,0:T(8,128)(2,1)S(1)}, u32[]{:S(2)}, u32[]{:S(2)}) collective-permute-start(bf16[1,64,1536]{2,1,0:T(8,128)(2,1)} %get-tuple-element.19), channel_id=1, source_target_pairs={{0,16},{2,18},{4,20},{6,22},{8,24},{10,26},{12,28},{14,30},{16,0},... | collective-permute-start | bytes 589832 | tf_op jit(solution)/shard_map/ppermute | solution.py:14
  263.5 5.5 %collective-permute-done.7 = bf16[1,64,1536]{2,1,0:T(8,128)(2,1)S(1)} collective-permute-done((bf16[1,64,1536]{2,1,0:T(8,128)(2,1)}, bf16[1,64,1536]{2,1,0:T(8,128)(2,1)S(1)}, u32[]{:S(2)}, u32[]{:S(2)}) %collective-permute-start.7) | collective-permute-done | bytes 196640 | tf_op jit(solution)/shard_map/ppermute | solution.py:14
  269.0 6.0 %collective-permute-start.8 = (bf16[1,64,1536]{2,1,0:T(8,128)(2,1)}, bf16[1,64,1536]{2,1,0:T(8,128)(2,1)S(1)}, u32[]{:S(2)}, u32[]{:S(2)}) collective-permute-start(bf16[1,64,1536]{2,1,0:T(8,128)(2,1)} %get-tuple-element.18), channel_id=1, source_target_pairs={{0,14},{2,16},{4,18},{6,20},{8,22},{10,24},{12,26},{14,28},{16,30}... | collective-permute-start | bytes 589832 | tf_op jit(solution)/shard_map/ppermute | solution.py:14
  275.1 5.5 %collective-permute-done.8 = bf16[1,64,1536]{2,1,0:T(8,128)(2,1)S(1)} collective-permute-done((bf16[1,64,1536]{2,1,0:T(8,128)(2,1)}, bf16[1,64,1536]{2,1,0:T(8,128)(2,1)S(1)}, u32[]{:S(2)}, u32[]{:S(2)}) %collective-permute-start.8) | collective-permute-done | bytes 196640 | tf_op jit(solution)/shard_map/ppermute | solution.py:14
  280.6 3.2 collective-permute-start.9
  283.8 8.5 %collective-permute-done.9 = bf16[1,64,1536]{2,1,0:T(8,128)(2,1)S(1)} collective-permute-done((bf16[1,64,1536]{2,1,0:T(8,128)(2,1)S(1)}, bf16[1,64,1536]{2,1,0:T(8,128)(2,1)S(1)}, u32[]{:S(2)}, u32[]{:S(2)}) %collective-permute-start.9) | collective-permute-done | bytes 196640 | tf_op jit(solution)/shard_map/ppermute | solution.py:14
  292.3 10.3 %collective-permute-done.10 = bf16[1,64,1536]{2,1,0:T(8,128)(2,1)S(1)} collective-permute-done((bf16[1,64,1536]{2,1,0:T(8,128)(2,1)S(1)}, bf16[1,64,1536]{2,1,0:T(8,128)(2,1)S(1)}, u32[]{:S(2)}, u32[]{:S(2)}) %collective-permute-start.10) | collective-permute-done | bytes 196640 | tf_op jit(solution)/shard_map/ppermute | solution.py:14
  302.8 0.9 slice_dynamic-update-slice_fusion
  303.7 2.8 fusion.16
  306.6 11.1 %convolution_convert_fusion = bf16[1024,1536]{1,0:T(8,128)(2,1)} fusion(bf16[1,768,1536]{2,1,0:T(8,128)(2,1)} %param.21, bf16[1024,1536]{1,0:T(8,128)(2,1)} %bitcast.116, bf16[1,1536,768]{2,1,0:T(8,128)(2,1)} %param.20), kind=kOutput, calls=%fused_computation.8 | convolution fusion | flops 4840488960 | bytes 11010048 | tf_op jit(solution)/shard_map/dot_general | solution.py:70
  317.7 4.6 %all-to-all-start.2 = ((bf16[16,64,1536]{2,1,0:T(8,128)(2,1)}), bf16[16,64,1536]{2,1,0:T(8,128)(2,1)}, u32[]{:S(2)}, u32[]{:S(2)}) async-start(bf16[16,64,1536]{2,1,0:T(8,128)(2,1)} %bitcast.115), calls=%async_computation.2 | async-start | bytes 6291456 | tf_op jit(solution)/shard_map/all_to_all | solution.py:132
  323.6 53.5 %all-to-all-done.2 = bf16[16,64,1536]{2,1,0:T(8,128)(2,1)} async-done(((bf16[16,64,1536]{2,1,0:T(8,128)(2,1)}), bf16[16,64,1536]{2,1,0:T(8,128)(2,1)}, u32[]{:S(2)}, u32[]{:S(2)}) %all-to-all-start.2) | async-done | bytes 3145760 | tf_op jit(solution)/shard_map/all_to_all | solution.py:132
  377.1 2.6 convert_reduce_fusion
  379.7 1.7 fusion.24
  381.5 26.3 %all-reduce.2.cloned.1.call-done = bf16[128,1536]{1,0:T(8,128)(2,1)} async-done(((bf16[128,1536]{1,0:T(8,128)(2,1)}), bf16[128,1536]{1,0:T(8,128)(2,1)}) %all-reduce.2.cloned.1.call-update) | async-done | bytes 393232 | tf_op jit(solution)/shard_map/psum | solution.py:21
  407.8 1.8 fusion.41
  (102 shorter events, 6.8 us)
Async XLA Ops:
  6.5 92.1 %copy-start = (bf16[1,768,1536]{2,1,0:T(8,128)(2,1)S(1)}, bf16[1,768,1536]{2,1,0:T(8,128)(2,1)}, u32[]{:S(2)}) copy-start(bf16[1,768,1536]{2,1,0:T(8,128)(2,1)} %param.19) | copy-start | bytes 7077892
  109.1 4.9 %copy-start.1 = (f32[1,128,1536]{2,1,0:T(8,128)S(1)}, f32[1,128,1536]{2,1,0:T(8,128)}, u32[]{:S(2)}) copy-start(f32[1,128,1536]{2,1,0:T(8,128)} %param.13) | copy-start | bytes 2359300
  109.1 4.9 %copy-start.8 = (f32[1536,4]{0,1:T(4,128)S(1)}, f32[1536,4]{0,1:T(4,128)}, u32[]{:S(2)}) copy-start(f32[1536,4]{0,1:T(4,128)} %param.22) | copy-start | bytes 73732
  109.1 5.4 %copy-start.12 = (s32[1,128,2]{1,2,0:T(2,128)S(1)}, s32[1,128,2]{1,2,0:T(2,128)}, u32[]{:S(2)}) copy-start(s32[1,128,2]{1,2,0:T(2,128)} %param.15) | copy-start | bytes 3076
  109.1 5.5 %copy-start.13 = (s32[128,2]{0,1:T(2,128)S(1)}, s32[128,2]{0,1:T(2,128)}, u32[]{:S(2)}) copy-start(s32[128,2]{0,1:T(2,128)} %param.16) | copy-start | bytes 3076
  109.1 64.8 %all-to-all-start.1 = ((bf16[16,64,1536]{2,1,0:T(8,128)(2,1)}), bf16[16,64,1536]{2,1,0:T(8,128)(2,1)}, u32[]{:S(2)}, u32[]{:S(2)}) async-start(bf16[16,64,1536]{2,1,0:T(8,128)(2,1)} %bitcast.114), calls=%async_computation.1 | async-start | bytes 6291456 | tf_op jit(solution)/shard_map/all_to_all | solution.py:124
  114.6 0.5 copy-start.10
  177.6 0.9 copy-start.3
  179.9 1.7 copy-start.2
  182.9 17.1 %collective-permute-start = (bf16[1,64,1536]{2,1,0:T(8,128)(2,1)}, bf16[1,64,1536]{2,1,0:T(8,128)(2,1)}, u32[]{:S(2)}, u32[]{:S(2)}) collective-permute-start(bf16[1,64,1536]{2,1,0:T(8,128)(2,1)} %get-tuple-element.26), channel_id=1, source_target_pairs={{0,30},{2,0},{4,2},{6,4},{8,6},{10,8},{12,10},{14,12},{16,14},{18,... | collective-permute-start | bytes 589832 | tf_op jit(solution)/shard_map/ppermute | solution.py:14
  195.4 85.1 %copy-start.6 = (bf16[1,64,1536]{2,1,0:T(8,128)(2,1)S(1)}, bf16[1,64,1536]{2,1,0:T(8,128)(2,1)}, u32[]{:S(2)}) copy-start(bf16[1,64,1536]{2,1,0:T(8,128)(2,1)} %get-tuple-element.17) | copy-start | bytes 589828
  195.5 96.9 %copy-start.5 = (bf16[1,64,1536]{2,1,0:T(8,128)(2,1)S(1)}, bf16[1,64,1536]{2,1,0:T(8,128)(2,1)}, u32[]{:S(2)}) copy-start(bf16[1,64,1536]{2,1,0:T(8,128)(2,1)} %get-tuple-element.16) | copy-start | bytes 589828
  195.5 107.3 %collective-permute-start.14 = (bf16[1,64,1536]{2,1,0:T(8,128)(2,1)S(1)}, bf16[1,64,1536]{2,1,0:T(8,128)(2,1)S(1)}, u32[]{:S(2)}, u32[]{:S(2)}) collective-permute-start(bf16[1,64,1536]{2,1,0:T(8,128)(2,1)S(1)} %get-tuple-element.12), channel_id=1, source_target_pairs={{0,2},{2,4},{4,6},{6,8},{8,10},{10,12},{12,14},{14,16},{16,18},{18... | collective-permute-start | bytes 589832 | tf_op jit(solution)/shard_map/ppermute | solution.py:14
  195.5 107.2 %collective-permute-start.13 = (bf16[1,64,1536]{2,1,0:T(8,128)(2,1)S(1)}, bf16[1,64,1536]{2,1,0:T(8,128)(2,1)S(1)}, u32[]{:S(2)}, u32[]{:S(2)}) collective-permute-start(bf16[1,64,1536]{2,1,0:T(8,128)(2,1)S(1)} %get-tuple-element.13), channel_id=1, source_target_pairs={{0,4},{2,6},{4,8},{6,10},{8,12},{10,14},{12,16},{14,18},{16,20},{1... | collective-permute-start | bytes 589832 | tf_op jit(solution)/shard_map/ppermute | solution.py:14
  195.5 107.2 %collective-permute-start.12 = (bf16[1,64,1536]{2,1,0:T(8,128)(2,1)S(1)}, bf16[1,64,1536]{2,1,0:T(8,128)(2,1)S(1)}, u32[]{:S(2)}, u32[]{:S(2)}) collective-permute-start(bf16[1,64,1536]{2,1,0:T(8,128)(2,1)S(1)} %get-tuple-element.14), channel_id=1, source_target_pairs={{0,6},{2,8},{4,10},{6,12},{8,14},{10,16},{12,18},{14,20},{16,22},{... | collective-permute-start | bytes 589832 | tf_op jit(solution)/shard_map/ppermute | solution.py:14
  198.1 104.6 %collective-permute-start.11 = (bf16[1,64,1536]{2,1,0:T(8,128)(2,1)S(1)}, bf16[1,64,1536]{2,1,0:T(8,128)(2,1)S(1)}, u32[]{:S(2)}, u32[]{:S(2)}) collective-permute-start(bf16[1,64,1536]{2,1,0:T(8,128)(2,1)S(1)} %get-tuple-element.15), channel_id=1, source_target_pairs={{0,8},{2,10},{4,12},{6,14},{8,16},{10,18},{12,20},{14,22},{16,24},... | collective-permute-start | bytes 589832 | tf_op jit(solution)/shard_map/ppermute | solution.py:14
  200.1 10.3 %collective-permute-start.1 = (bf16[1,64,1536]{2,1,0:T(8,128)(2,1)}, bf16[1,64,1536]{2,1,0:T(8,128)(2,1)S(1)}, u32[]{:S(2)}, u32[]{:S(2)}) collective-permute-start(bf16[1,64,1536]{2,1,0:T(8,128)(2,1)} %get-tuple-element.25), channel_id=1, source_target_pairs={{0,28},{2,30},{4,0},{6,2},{8,4},{10,6},{12,8},{14,10},{16,12},{18,... | collective-permute-start | bytes 589832 | tf_op jit(solution)/shard_map/ppermute | solution.py:14
  210.4 8.7 %collective-permute-start.2 = (bf16[1,64,1536]{2,1,0:T(8,128)(2,1)}, bf16[1,64,1536]{2,1,0:T(8,128)(2,1)S(1)}, u32[]{:S(2)}, u32[]{:S(2)}) collective-permute-start(bf16[1,64,1536]{2,1,0:T(8,128)(2,1)} %get-tuple-element.24), channel_id=1, source_target_pairs={{0,26},{2,28},{4,30},{6,0},{8,2},{10,4},{12,6},{14,8},{16,10},{18,... | collective-permute-start | bytes 589832 | tf_op jit(solution)/shard_map/ppermute | solution.py:14
  219.1 6.2 %collective-permute-start.3 = (bf16[1,64,1536]{2,1,0:T(8,128)(2,1)}, bf16[1,64,1536]{2,1,0:T(8,128)(2,1)S(1)}, u32[]{:S(2)}, u32[]{:S(2)}) collective-permute-start(bf16[1,64,1536]{2,1,0:T(8,128)(2,1)} %get-tuple-element.23), channel_id=1, source_target_pairs={{0,24},{2,26},{4,28},{6,30},{8,0},{10,2},{12,4},{14,6},{16,8},{18,... | collective-permute-start | bytes 589832 | tf_op jit(solution)/shard_map/ppermute | solution.py:14
  225.2 6.8 %collective-permute-start.4 = (bf16[1,64,1536]{2,1,0:T(8,128)(2,1)}, bf16[1,64,1536]{2,1,0:T(8,128)(2,1)S(1)}, u32[]{:S(2)}, u32[]{:S(2)}) collective-permute-start(bf16[1,64,1536]{2,1,0:T(8,128)(2,1)} %get-tuple-element.22), channel_id=1, source_target_pairs={{0,22},{2,24},{4,26},{6,28},{8,30},{10,0},{12,2},{14,4},{16,6},{18... | collective-permute-start | bytes 589832 | tf_op jit(solution)/shard_map/ppermute | solution.py:14
  232.0 7.2 %collective-permute-start.5 = (bf16[1,64,1536]{2,1,0:T(8,128)(2,1)}, bf16[1,64,1536]{2,1,0:T(8,128)(2,1)S(1)}, u32[]{:S(2)}, u32[]{:S(2)}) collective-permute-start(bf16[1,64,1536]{2,1,0:T(8,128)(2,1)} %get-tuple-element.21), channel_id=1, source_target_pairs={{0,20},{2,22},{4,24},{6,26},{8,28},{10,30},{12,0},{14,2},{16,4},{1... | collective-permute-start | bytes 589832 | tf_op jit(solution)/shard_map/ppermute | solution.py:14
  239.2 17.2 %collective-permute-start.6 = (bf16[1,64,1536]{2,1,0:T(8,128)(2,1)}, bf16[1,64,1536]{2,1,0:T(8,128)(2,1)S(1)}, u32[]{:S(2)}, u32[]{:S(2)}) collective-permute-start(bf16[1,64,1536]{2,1,0:T(8,128)(2,1)} %get-tuple-element.20), channel_id=1, source_target_pairs={{0,18},{2,20},{4,22},{6,24},{8,26},{10,28},{12,30},{14,0},{16,2},{... | collective-permute-start | bytes 589832 | tf_op jit(solution)/shard_map/ppermute | solution.py:14
  256.4 12.6 %collective-permute-start.7 = (bf16[1,64,1536]{2,1,0:T(8,128)(2,1)}, bf16[1,64,1536]{2,1,0:T(8,128)(2,1)S(1)}, u32[]{:S(2)}, u32[]{:S(2)}) collective-permute-start(bf16[1,64,1536]{2,1,0:T(8,128)(2,1)} %get-tuple-element.19), channel_id=1, source_target_pairs={{0,16},{2,18},{4,20},{6,22},{8,24},{10,26},{12,28},{14,30},{16,0},... | collective-permute-start | bytes 589832 | tf_op jit(solution)/shard_map/ppermute | solution.py:14
  269.0 11.6 %collective-permute-start.8 = (bf16[1,64,1536]{2,1,0:T(8,128)(2,1)}, bf16[1,64,1536]{2,1,0:T(8,128)(2,1)S(1)}, u32[]{:S(2)}, u32[]{:S(2)}) collective-permute-start(bf16[1,64,1536]{2,1,0:T(8,128)(2,1)} %get-tuple-element.18), channel_id=1, source_target_pairs={{0,14},{2,16},{4,18},{6,20},{8,22},{10,24},{12,26},{14,28},{16,30}... | collective-permute-start | bytes 589832 | tf_op jit(solution)/shard_map/ppermute | solution.py:14
  280.6 11.7 %collective-permute-start.9 = (bf16[1,64,1536]{2,1,0:T(8,128)(2,1)S(1)}, bf16[1,64,1536]{2,1,0:T(8,128)(2,1)S(1)}, u32[]{:S(2)}, u32[]{:S(2)}) collective-permute-start(bf16[1,64,1536]{2,1,0:T(8,128)(2,1)S(1)} %copy-done.6), channel_id=1, source_target_pairs={{0,12},{2,14},{4,16},{6,18},{8,20},{10,22},{12,24},{14,26},{16,28}... | collective-permute-start | bytes 589832 | tf_op jit(solution)/shard_map/ppermute | solution.py:14
  292.3 10.3 %collective-permute-start.10 = (bf16[1,64,1536]{2,1,0:T(8,128)(2,1)S(1)}, bf16[1,64,1536]{2,1,0:T(8,128)(2,1)S(1)}, u32[]{:S(2)}, u32[]{:S(2)}) collective-permute-start(bf16[1,64,1536]{2,1,0:T(8,128)(2,1)S(1)} %copy-done.5), channel_id=1, source_target_pairs={{0,10},{2,12},{4,14},{6,16},{8,18},{10,20},{12,22},{14,24},{16,26}... | collective-permute-start | bytes 589832 | tf_op jit(solution)/shard_map/ppermute | solution.py:14
  317.7 5.3 %copy-start.9 = (f32[1536,4]{0,1:T(4,128)S(1)}, f32[1536,4]{0,1:T(4,128)}, u32[]{:S(2)}) copy-start(f32[1536,4]{0,1:T(4,128)} %param.23) | copy-start | bytes 73732
  317.7 5.7 %copy-start.14 = (s32[128,2]{0,1:T(2,128)S(1)}, s32[128,2]{0,1:T(2,128)}, u32[]{:S(2)}) copy-start(s32[128,2]{0,1:T(2,128)} %param.16) | copy-start | bytes 3076
  317.7 5.8 %copy-start.11 = (pred[128,2,4]{0,2,1:T(4,128)(4,1)S(1)}, pred[128,2,4]{0,2,1:T(4,128)(4,1)}, u32[]{:S(2)}) copy-start(pred[128,2,4]{0,2,1:T(4,128)(4,1)} %copy-done.10) | copy-start | bytes 3076
  317.7 59.4 %all-to-all-start.2 = ((bf16[16,64,1536]{2,1,0:T(8,128)(2,1)}), bf16[16,64,1536]{2,1,0:T(8,128)(2,1)}, u32[]{:S(2)}, u32[]{:S(2)}) async-start(bf16[16,64,1536]{2,1,0:T(8,128)(2,1)} %bitcast.115), calls=%async_computation.2 | async-start | bytes 6291456 | tf_op jit(solution)/shard_map/all_to_all | solution.py:132
  322.3 57.4 %copy-start.7 = (f32[1536]{0:T(1024)S(1)}, f32[1536]{0:T(1024)}, u32[]{:S(2)}) copy-start(f32[1536]{0:T(1024)} %get-tuple-element.6) | copy-start | bytes 18436
  322.3 85.4 %all-reduce.2.cloned.1.call-start = ((), (), s32[]{:S(2)}) async-start(), calls=%async_computation.3 | async-start | bytes 786432 | tf_op jit(solution)/shard_map/psum | solution.py:21
  323.6 84.2 %copy-start.4 = (f32[128,1536]{1,0:T(8,128)S(1)}, f32[128,1536]{1,0:T(8,128)}, u32[]{:S(2)}) copy-start(f32[128,1536]{1,0:T(8,128)} %copy-done.3) | copy-start | bytes 2359300
Sparse Core Ops, SparseCore 0:
  381.6 26.1 all-reduce.1
